TPU v7x, 512 devices: a whole 4x8x8 slice. The times are simulated.
512 devices in a mesh: leaf: 8 (over x, core), front: 64 (over y, z).
Axes of the slice: x: 4, y: 8, z: 8, core: 2. Of those that a mesh axis runs over, the one named last changes fastest.
Arguments:
- rhs_leaf: float32 [8, 32, 229376], P('leaf', None, 'front'), may hold values from -6 to 6
- rhs_sep: float32 [8, 32, 8192], P('leaf', None, 'front'), may hold values from -6 to 6
- leaf_inv: float32 [8, 1792, 128, 128], P('leaf', 'front')
- leaf_update: float32 [8, 1792, 128, 128], P('leaf', 'front'), may hold values from -0.09375 to 0.09375
- update_rows: int32 [8, 1792, 128], P('leaf', 'front'), may hold values from 0 to 128, as said below
- update_owner: int32 [8, 1792, 1], P('leaf', 'front'), may hold values from 0 to 63; in each aligned block of 28 rows (0 to 27, 28 to 55, ..., all dimensions but the last counted through in order) no two rows name the same one
- sep_inv: float32 [8, 64, 128, 128], P('leaf', 'front')
- sep_couple: float32 [8, 64, 128, 128], P('leaf', 'front'), may hold values from -0.375 to 0.375
Outputs:
- x_leaf: float32 [8, 32, 229376], P('leaf', None, 'front')
- x_sep: float32 [8, 32, 8192], P('leaf', None, 'front')
Inputs may be any that keep to these rules, and one draw needn't show every extreme that they name: `update_rows`: within each leaf front the entries below 128 are distinct; the entries equal to 128 mark padded rows and come last in the front; some front has 64 padded rows. `update_owner`: at most 1 of the 28 leaf fronts held by one index of front have the same owner, and some index of front reaches 1.
All inputs are finite; a program needn't handle non-finite values.
Results may differ from a plain program's by a relative error of at most 0.0001.
Values sent between devices are 32-bit elements; how exact they have to be, the bound alone decides.
No kernel may reach another device: no remote copies, remote signals or barrier semaphores. Data moves between devices by JAX's collectives and lax.ppermute only.
A program may use at most 64 MiB of HBM per device.

v0:
```python
import jax
import jax.numpy as jnp
from jax import lax
from jax.sharding import PartitionSpec as P


def from_behind(value, axis, steps):
    count = lax.axis_size(axis)
    initial, last = (max(0, -steps), min(count, count - steps))
    return lax.ppermute(value, axis, [(source, source + steps) for source in range(initial, last)])


def apply_blocks(matrices, vectors):
    return jnp.einsum("bik,rbk->rbi", matrices, vectors, precision=lax.Precision.HIGHEST)


def apply_transposed(matrices, vectors):
    return jnp.einsum("bki,rbk->rbi", matrices, vectors, precision=lax.Precision.HIGHEST)


def apply_map(matrix, vectors):
    return jnp.einsum("ik,rk->ri", matrix, vectors, precision=lax.Precision.HIGHEST)


def apply_map_transposed(matrix, vectors):
    return jnp.einsum("ki,rk->ri", matrix, vectors, precision=lax.Precision.HIGHEST)


def per_device(
    rhs_leaf, rhs_sep, leaf_inv, leaf_update, update_rows, update_owner, sep_inv, sep_couple
):
    block_rows = leaf_inv.shape[-1]
    front_count = leaf_inv.shape[1]
    rhs_count = rhs_leaf.shape[1]
    fronts = lax.axis_size("front")
    groups = lax.axis_size("leaf")
    right_leaf = rhs_leaf[0].reshape(rhs_count, front_count, block_rows)
    leaf_y = apply_blocks(leaf_inv[0], right_leaf)
    updates = apply_blocks(leaf_update[0], leaf_y)
    row_index = update_rows[0]
    owners = update_owner[0]
    live_mask = row_index < block_rows
    updates = jnp.where(live_mask[None], updates, 0.0)
    local_rows = jnp.minimum(row_index, block_rows - 1)
    targets = owners * block_rows + local_rows
    dense_term = jnp.zeros((rhs_count, fronts * block_rows), jnp.float32)
    dense_term = dense_term.at[:, targets.reshape(-1)].add(updates.reshape(rhs_count, -1))
    collected = lax.psum_scatter(dense_term, "front", scatter_dimension=1, tiled=True)
    reduced = rhs_sep[0] - collected
    inv_block = sep_inv[0, 0]
    couple = sep_couple[0, 0]

    def forward_turn(turn_index, current):
        before = from_behind(current, "leaf", 1)
        return apply_map(inv_block, reduced - apply_map(couple, before))

    solved = lax.fori_loop(0, groups - 1, forward_turn, apply_map(inv_block, reduced))

    def backward_turn(turn_index, current):
        coupled = apply_map_transposed(couple, current)
        after = from_behind(coupled, "leaf", -1)
        return apply_map_transposed(inv_block, solved - after)

    x_sep = lax.fori_loop(0, groups - 1, backward_turn, apply_map_transposed(inv_block, solved))
    gathered = lax.all_gather(x_sep, "front", axis=1, tiled=True)
    picked = jnp.take(gathered, targets.reshape(-1), axis=1).reshape(
        rhs_count, front_count, block_rows
    )
    picked = jnp.where(live_mask[None], picked, 0.0)
    residue = leaf_y - apply_transposed(leaf_update[0], picked)
    x_leaf = apply_transposed(leaf_inv[0], residue)
    return (x_leaf.reshape(1, rhs_count, front_count * block_rows), x_sep[None])


def solution(mesh):
    placed = (
        P("leaf", None, "front"),
        P("leaf", None, "front"),
        P("leaf", "front", None, None),
        P("leaf", "front", None, None),
        P("leaf", "front", None),
        P("leaf", "front", None),
        P("leaf", "front", None, None),
        P("leaf", "front", None, None),
    )
    return jax.shard_map(
        per_device,
        mesh=mesh,
        in_specs=placed,
        out_specs=(P("leaf", None, "front"), P("leaf", None, "front")),
        check_vma=False,
    )
```

profile of v0, /device:TPU:2, one launch (start us, length us, event | category | flops | bytes accessed | tf_op | source)
XLA Modules:
  0.0 480.7 jit_solution(9119982957623492532)
XLA Ops:
  7.2 1.2 reshape_squeeze.3
  8.5 0.7 broadcast_compare_fusion
  9.2 4.4 fusion.14
  13.7 3.0 fusion.28
  16.7 1.8 copy.17
  18.6 23.0 %scatter_custom_fusion = f32[32,8192]{0,1:T(8,128)} fusion(s32[3584]{0:T(1024)S(1)} %fusion.41, f32[3584,32]{1,0:T(8,128)} %copy.17, f32[]{:T(128)} %constant.20.clone.1), kind=kCustom, calls=%fused_computation.5 | custom fusion | flops 114688 | bytes 1049088 | tf_op jit(solution)/shard_map/scatter-add | solution.py:47
  41.7 0.6 copy-done.6
  42.4 251.3 %reduce-scatter.2.cloned.1.call-done = f32[32,128]{0,1:T(8,128)} async-done(((f32[32,8192]{0,1:T(8,128)}), f32[32,128]{0,1:T(8,128)}) %reduce-scatter.2.cloned.1.call-update) | async-done | bytes 16400 | tf_op jit(solution)/shard_map/reduce_scatter | solution.py:48
  293.7 0.8 bitcast_subtract_fusion
  294.6 0.2 fusion.44
  294.9 38.5 %while.20 = (s32[]{:T(128)}, f32[32,128]{1,0:T(8,128)S(1)}, f32[128,128]{1,0:T(8,128)S(1)}, f32[32,128]{1,0:T(8,128)S(1)}, f32[128,128]{1,0:T(8,128)S(1)}, /*index=5*/s32[]{:T(128)}) while((s32[]{:T(128)}, f32[32,128]{1,0:T(8,128)S(1)}, f32[128,128]{1,0:T(8,128)S(1)}, f32[32,128]{1,0:T(8,128)S(1)}, f32[128,128]{1,0:T(8,128)S(1)}, ...), condition=%wide.region_3.4_spmd, body=%wide.region_2.3_spmd.sunk | while | flops 12587010 | bytes 278637 | solution.py:57
  294.9 1.9 collective-permute-start
  296.8 3.1 collective-permute-done
  300.4 1.9 collective-permute-start
  302.3 3.1 collective-permute-done
  305.9 1.9 collective-permute-start
  307.8 3.1 collective-permute-done
  311.4 1.9 collective-permute-start
  313.3 3.1 collective-permute-done
  316.6 0.2 fusion.76
  316.9 1.9 collective-permute-start
  318.8 3.1 collective-permute-done
  322.4 1.9 collective-permute-start
  324.3 3.1 collective-permute-done
  327.9 1.9 collective-permute-start
  329.8 3.1 collective-permute-done
  333.5 36.1 %while.21 = (s32[]{:T(128)}, f32[32,128]{1,0:T(8,128)S(1)}, f32[128,128]{1,0:T(8,128)S(1)}, f32[32,128]{1,0:T(8,128)S(1)}, f32[128,128]{1,0:T(8,128)S(1)}, /*index=5*/s32[]{:T(128)}) while((s32[]{:T(128)}, f32[32,128]{1,0:T(8,128)S(1)}, f32[128,128]{1,0:T(8,128)S(1)}, f32[32,128]{1,0:T(8,128)S(1)}, f32[128,128]{1,0:T(8,128)S(1)}, ...), condition=%wide.region_5.6_spmd, body=%wide.region_4.5_spmd.sunk | while | flops 12587010 | bytes 278637 | solution.py:64
  333.7 1.9 collective-permute-start.1
  335.6 1.4 collective-permute-done.1
  337.4 3.6 collective-permute-start.1
  341.0 1.4 collective-permute-done.1
  342.8 3.6 collective-permute-start.1
  346.4 1.4 collective-permute-done.1
  348.2 3.6 collective-permute-start.1
  351.8 1.4 collective-permute-done.1
  353.6 3.6 collective-permute-start.1
  357.2 1.4 collective-permute-done.1
  359.0 3.6 collective-permute-start.1
  362.6 1.4 collective-permute-done.1
  364.4 3.6 collective-permute-start.1
  368.0 1.4 collective-permute-done.1
  369.6 0.7 copy.19
  370.5 85.2 %all-gather.2.cloned.1.call-done = f32[32,8192]{0,1:T(8,128)} async-done(((f32[32,128]{0,1:T(8,128)}), f32[32,8192]{0,1:T(8,128)}) %all-gather.2.cloned.1.call-update) | async-done | bytes 1048592 | tf_op jit(solution)/shard_map/all_gather | solution.py:65
  455.7 9.5 %gather_fusion = f32[3584,32]{1,0:T(8,128)} fusion(f32[32,8192]{0,1:T(8,128)} %all-gather.2.cloned.1.call-done, s32[4096]{0:T(1024)S(1)} %pad_clamp_fusion), kind=kCustom, calls=%fused_computation | custom fusion | bytes 931840 | tf_op jit(solution)/shard_map/jit(_take)/gather | solution.py:66
  465.2 5.8 %fusion.31 = f32[32,28,128]{2,0,1:T(8,128)S(1)} fusion(f32[32,28,128]{2,0,1:T(8,128)S(1)} %fusion.14, f32[1,28,128,128]{3,2,1,0:T(8,128)S(1)} %copy-done, f32[32,28,128]{0,2,1:T(8,128)} %bitcast.100, pred[28,128]{1,0:T(8,128)(4,1)S(1)} %compare_and_fusion, pred[28,128]{1,0:T(8,128)(4,1)S(1)} %bitcast.104), kind=kOutput, calls=%fused_computation.22 | convolution fusion | flops 176504832 | bytes 3218432 | tf_op jit(solution)/shard_map/bki,rbk->rbi/dot_general | solution.py:18
  471.0 1.7 fusion.17
  472.8 0.3 copy.20
  473.0 0.8 reshape.72
  (57 shorter events, 5.5 us)
Async XLA Ops:
  7.2 6.5 %copy-start = (f32[1,28,128,128]{3,2,1,0:T(8,128)S(1)}, f32[1,28,128,128]{3,2,1,0:T(8,128)}, u32[]{:S(2)}) copy-start(f32[1,28,128,128]{3,2,1,0:T(8,128)} %param.15) | copy-start | bytes 5505028
  7.2 286.5 %reduce-scatter.2.cloned.1.call-start = ((), (), s32[]{:S(2)}) async-start(), calls=%async_computation.1 | async-start | bytes 4259840 | tf_op jit(solution)/shard_map/reduce_scatter | solution.py:48
  16.6 1.9 copy-start.7
  16.6 1.9 copy-start.5
  41.6 0.7 copy-start.6
  41.6 253.0 %copy-start.1 = (f32[1,1,128,128]{3,2,1,0:T(8,128)S(1)}, f32[1,1,128,128]{3,2,1,0:T(8,128)}, u32[]{:S(2)}) copy-start(f32[1,1,128,128]{3,2,1,0:T(8,128)} %param.18) | copy-start | bytes 196612
  41.6 253.2 %copy-start.3 = (f32[1,1,128,128]{3,2,1,0:T(8,128)S(1)}, f32[1,1,128,128]{3,2,1,0:T(8,128)}, u32[]{:S(2)}) copy-start(f32[1,1,128,128]{3,2,1,0:T(8,128)} %param.19) | copy-start | bytes 196612
  41.6 414.1 %all-gather.2.cloned.1.call-start = ((), (), s32[]{:S(2)}) async-start(), calls=%async_computation.2 | async-start | bytes 4259840 | tf_op jit(solution)/shard_map/all_gather | solution.py:65
  294.9 5.1 %collective-permute-start = (f32[32,128]{1,0:T(8,128)S(1)}, f32[32,128]{1,0:T(8,128)S(1)}, u32[]{:S(2)}, u32[]{:S(2)}) collective-permute-start(f32[32,128]{1,0:T(8,128)S(1)} %get-tuple-element.157), channel_id=1, source_target_pairs={{0,64},{64,128},{128,192},{192,256},{256,320},{320,384},{384,448},... | collective-permute-start | bytes 49160 | tf_op jit(solution)/shard_map/while/body/eval_jaxpr/ppermute | solution.py:10
  300.4 5.1 %collective-permute-start = (f32[32,128]{1,0:T(8,128)S(1)}, f32[32,128]{1,0:T(8,128)S(1)}, u32[]{:S(2)}, u32[]{:S(2)}) collective-permute-start(f32[32,128]{1,0:T(8,128)S(1)} %get-tuple-element.157), channel_id=1, source_target_pairs={{0,64},{64,128},{128,192},{192,256},{256,320},{320,384},{384,448},... | collective-permute-start | bytes 49160 | tf_op jit(solution)/shard_map/while/body/eval_jaxpr/ppermute | solution.py:10
  305.9 5.1 %collective-permute-start = (f32[32,128]{1,0:T(8,128)S(1)}, f32[32,128]{1,0:T(8,128)S(1)}, u32[]{:S(2)}, u32[]{:S(2)}) collective-permute-start(f32[32,128]{1,0:T(8,128)S(1)} %get-tuple-element.157), channel_id=1, source_target_pairs={{0,64},{64,128},{128,192},{192,256},{256,320},{320,384},{384,448},... | collective-permute-start | bytes 49160 | tf_op jit(solution)/shard_map/while/body/eval_jaxpr/ppermute | solution.py:10
  311.4 5.1 %collective-permute-start = (f32[32,128]{1,0:T(8,128)S(1)}, f32[32,128]{1,0:T(8,128)S(1)}, u32[]{:S(2)}, u32[]{:S(2)}) collective-permute-start(f32[32,128]{1,0:T(8,128)S(1)} %get-tuple-element.157), channel_id=1, source_target_pairs={{0,64},{64,128},{128,192},{192,256},{256,320},{320,384},{384,448},... | collective-permute-start | bytes 49160 | tf_op jit(solution)/shard_map/while/body/eval_jaxpr/ppermute | solution.py:10
  316.9 5.1 %collective-permute-start = (f32[32,128]{1,0:T(8,128)S(1)}, f32[32,128]{1,0:T(8,128)S(1)}, u32[]{:S(2)}, u32[]{:S(2)}) collective-permute-start(f32[32,128]{1,0:T(8,128)S(1)} %get-tuple-element.157), channel_id=1, source_target_pairs={{0,64},{64,128},{128,192},{192,256},{256,320},{320,384},{384,448},... | collective-permute-start | bytes 49160 | tf_op jit(solution)/shard_map/while/body/eval_jaxpr/ppermute | solution.py:10
  322.4 5.1 %collective-permute-start = (f32[32,128]{1,0:T(8,128)S(1)}, f32[32,128]{1,0:T(8,128)S(1)}, u32[]{:S(2)}, u32[]{:S(2)}) collective-permute-start(f32[32,128]{1,0:T(8,128)S(1)} %get-tuple-element.157), channel_id=1, source_target_pairs={{0,64},{64,128},{128,192},{192,256},{256,320},{320,384},{384,448},... | collective-permute-start | bytes 49160 | tf_op jit(solution)/shard_map/while/body/eval_jaxpr/ppermute | solution.py:10
  327.9 5.1 %collective-permute-start = (f32[32,128]{1,0:T(8,128)S(1)}, f32[32,128]{1,0:T(8,128)S(1)}, u32[]{:S(2)}, u32[]{:S(2)}) collective-permute-start(f32[32,128]{1,0:T(8,128)S(1)} %get-tuple-element.157), channel_id=1, source_target_pairs={{0,64},{64,128},{128,192},{192,256},{256,320},{320,384},{384,448},... | collective-permute-start | bytes 49160 | tf_op jit(solution)/shard_map/while/body/eval_jaxpr/ppermute | solution.py:10
  333.7 3.4 collective-permute-start.1
  337.4 5.1 %collective-permute-start.1 = (f32[32,128]{1,0:T(8,128)S(1)}, f32[32,128]{1,0:T(8,128)S(1)}, u32[]{:S(2)}, u32[]{:S(2)}) collective-permute-start(f32[32,128]{1,0:T(8,128)S(1)} %fusion.81), channel_id=1, source_target_pairs={{64,0},{128,64},{192,128},{256,192},{320,256},{384,320},{448,384},... | collective-permute-start | bytes 49160 | tf_op jit(solution)/shard_map/while/body/eval_jaxpr/ppermute | solution.py:10
  342.8 5.1 %collective-permute-start.1 = (f32[32,128]{1,0:T(8,128)S(1)}, f32[32,128]{1,0:T(8,128)S(1)}, u32[]{:S(2)}, u32[]{:S(2)}) collective-permute-start(f32[32,128]{1,0:T(8,128)S(1)} %fusion.81), channel_id=1, source_target_pairs={{64,0},{128,64},{192,128},{256,192},{320,256},{384,320},{448,384},... | collective-permute-start | bytes 49160 | tf_op jit(solution)/shard_map/while/body/eval_jaxpr/ppermute | solution.py:10
  348.2 5.1 %collective-permute-start.1 = (f32[32,128]{1,0:T(8,128)S(1)}, f32[32,128]{1,0:T(8,128)S(1)}, u32[]{:S(2)}, u32[]{:S(2)}) collective-permute-start(f32[32,128]{1,0:T(8,128)S(1)} %fusion.81), channel_id=1, source_target_pairs={{64,0},{128,64},{192,128},{256,192},{320,256},{384,320},{448,384},... | collective-permute-start | bytes 49160 | tf_op jit(solution)/shard_map/while/body/eval_jaxpr/ppermute | solution.py:10
  353.6 5.1 %collective-permute-start.1 = (f32[32,128]{1,0:T(8,128)S(1)}, f32[32,128]{1,0:T(8,128)S(1)}, u32[]{:S(2)}, u32[]{:S(2)}) collective-permute-start(f32[32,128]{1,0:T(8,128)S(1)} %fusion.81), channel_id=1, source_target_pairs={{64,0},{128,64},{192,128},{256,192},{320,256},{384,320},{448,384},... | collective-permute-start | bytes 49160 | tf_op jit(solution)/shard_map/while/body/eval_jaxpr/ppermute | solution.py:10
  359.0 5.1 %collective-permute-start.1 = (f32[32,128]{1,0:T(8,128)S(1)}, f32[32,128]{1,0:T(8,128)S(1)}, u32[]{:S(2)}, u32[]{:S(2)}) collective-permute-start(f32[32,128]{1,0:T(8,128)S(1)} %fusion.81), channel_id=1, source_target_pairs={{64,0},{128,64},{192,128},{256,192},{320,256},{384,320},{448,384},... | collective-permute-start | bytes 49160 | tf_op jit(solution)/shard_map/while/body/eval_jaxpr/ppermute | solution.py:10
  364.4 5.1 %collective-permute-start.1 = (f32[32,128]{1,0:T(8,128)S(1)}, f32[32,128]{1,0:T(8,128)S(1)}, u32[]{:S(2)}, u32[]{:S(2)}) collective-permute-start(f32[32,128]{1,0:T(8,128)S(1)} %fusion.81), channel_id=1, source_target_pairs={{64,0},{128,64},{192,128},{256,192},{320,256},{384,320},{448,384},... | collective-permute-start | bytes 49160 | tf_op jit(solution)/shard_map/while/body/eval_jaxpr/ppermute | solution.py:10
  369.6 95.6 %copy-start.4 = (f32[32,128]{1,0:T(8,128)}, f32[32,128]{1,0:T(8,128)S(1)}, u32[]{:S(2)}) copy-start(f32[32,128]{1,0:T(8,128)S(1)} %get-tuple-element.57) | copy-start | bytes 49156
  465.2 5.8 %copy-start.2 = (f32[1,28,128,128]{3,2,1,0:T(8,128)S(1)}, f32[1,28,128,128]{3,2,1,0:T(8,128)}, u32[]{:S(2)}) copy-start(f32[1,28,128,128]{3,2,1,0:T(8,128)} %param.14) | copy-start | bytes 5505028
Sparse Core Ops, SparseCore 0:
  41.7 251.8 reduce-scatter.1
  370.5 85.1 all-gather.1
where the time goes:
time: 481 us
  waiting for transfers between devices  368 us (77%)
  starting transfers between devices  37.2 us (8%)
  other arithmetic  24.7 us (5%)
  matrix products  20.3 us (4%)
  local copies, waits for them, and re-layouts  15.4 us (3%)
  between operations  14.2 us (3%)
    reduce_scatter x1, waiting for transfers between devices, per_device(): lax.psum_scatter(dense_term, 'front', scatter_dimension=1, tiled=True)  251 us
    all_gather x1, waiting for transfers between devices, per_device(): gathered = lax.all_gather(x_sep, 'front', axis=1, tiled=True)  85.2 us
    ppermute x14, starting transfers between devices, from_behind(): lax.ppermute(value, axis, [(source, source + steps) for source in range(i...  37.2 us
    ppermute x14, waiting for transfers between devices, from_behind(): lax.ppermute(value, axis, [(source, source + steps) for source in range(i...  31.9 us
    scatter-add x1, other arithmetic, per_device(): dense_term.at[:, targets.reshape(-1)].add(updates.reshape(rhs_count, -1))  23 us
  transfers between devices with their start and end apart: 16, of which 16 were waited for; matrix products, arithmetic and copies ran while one was open for 0% of the time, Pallas kernels for 0%

commit v1 on v0

--- a/solution.py
+++ b/solution.py
@@ -62,7 +62,9 @@
         return apply_map_transposed(inv_block, solved - after)
 
     x_sep = lax.fori_loop(0, groups - 1, backward_turn, apply_map_transposed(inv_block, solved))
-    gathered = lax.all_gather(x_sep, "front", axis=1, tiled=True)
+    gathered = jnp.concatenate(
+        lax.all_to_all(jnp.stack([x_sep] * lax.axis_size("front")), "front", 0, 0), axis=1
+    )
     picked = jnp.take(gathered, targets.reshape(-1), axis=1).reshape(
         rhs_count, front_count, block_rows
     )

time: 481 us -> 438 us (0.911)
  the two profiles are of different devices: /device:TPU:2 before, /device:TPU:21 now
where the time goes in v1:
time: 438 us; the launch traced here: 437 us
  waiting for transfers between devices  304 us (69%)
  starting transfers between devices  57.2 us (13%)
  other arithmetic  24.7 us (6%)
  local copies, waits for them, and re-layouts  20.5 us (5%)
  matrix products  16.2 us (4%)
  between operations  14.2 us (3%)
    reduce_scatter x1, waiting for transfers between devices, per_device(): lax.psum_scatter(dense_term, 'front', scatter_dimension=1, tiled=True)  246 us
    ppermute x14, starting transfers between devices, from_behind(): lax.ppermute(value, axis, [(source, source + steps) for source in range(i...  48.5 us
    all_to_all x1, waiting for transfers between devices, per_device(): lax.all_to_all(jnp.stack([x_sep] * lax.axis_size('front')), 'front', 0, 0)  30.5 us
    ppermute x14, waiting for transfers between devices, from_behind(): lax.ppermute(value, axis, [(source, source + steps) for source in range(i...  26.9 us
    scatter-add x1, other arithmetic, per_device(): dense_term.at[:, targets.reshape(-1)].add(updates.reshape(rhs_count, -1))  22.9 us
    gather x2, local copies, waits for them, and re-layouts, per_device(): jnp.take(gathered, targets.reshape(-1), axis=1)  11.6 us
  transfers between devices with their start and end apart: 16, of which 16 were waited for; matrix products, arithmetic and copies ran while one was open for 0% of the time, Pallas kernels for 0%

profile of v1, /device:TPU:21, one launch (start us, length us, event | category | flops | bytes accessed | tf_op | source)
XLA Modules:
  0.0 436.8 jit_solution(10685243955041255400)
XLA Ops:
  7.2 1.2 reshape_squeeze.3
  8.5 0.7 broadcast_compare_fusion
  9.2 4.4 %fusion.12 = f32[32,28,128]{2,0,1:T(8,128)S(1)} fusion(f32[1,28,128,128]{3,2,1,0:T(8,128)} %param.14, f32[32,28,128]{2,1,0:T(8,128)S(1)} %reshape_squeeze.3), kind=kOutput, calls=%fused_computation.15 | convolution fusion | flops 176160768 | bytes 2752512 | tf_op jit(solution)/shard_map/bik,rbk->rbi/dot_general | solution.py:14
  13.7 3.0 fusion.27
  16.7 1.8 copy.24
  18.6 22.9 %scatter_custom_fusion = f32[32,8192]{0,1:T(8,128)} fusion(s32[3584]{0:T(1024)S(1)} %fusion.37, f32[3584,32]{1,0:T(8,128)} %copy.24, f32[]{:T(128)} %constant.20.clone.1), kind=kCustom, calls=%fused_computation.5 | custom fusion | flops 114688 | bytes 1049088 | tf_op jit(solution)/shard_map/scatter-add | solution.py:47
  41.6 0.7 copy-done.6
  42.4 246.1 %reduce-scatter.2.cloned.1.call-done = f32[32,128]{0,1:T(8,128)} async-done(((f32[32,8192]{0,1:T(8,128)}), f32[32,128]{0,1:T(8,128)}) %reduce-scatter.2.cloned.1.call-update) | async-done | bytes 16400 | tf_op jit(solution)/shard_map/reduce_scatter | solution.py:48
  288.5 0.8 bitcast_subtract_fusion
  289.7 42.6 %while.20 = (s32[]{:T(128)}, f32[32,128]{1,0:T(8,128)S(1)}, f32[128,128]{1,0:T(8,128)S(1)}, f32[32,128]{1,0:T(8,128)S(1)}, f32[128,128]{1,0:T(8,128)S(1)}, /*index=5*/s32[]{:T(128)}) while((s32[]{:T(128)}, f32[32,128]{1,0:T(8,128)S(1)}, f32[128,128]{1,0:T(8,128)S(1)}, f32[32,128]{1,0:T(8,128)S(1)}, f32[128,128]{1,0:T(8,128)S(1)}, ...), condition=%wide.region_3.4_spmd, body=%wide.region_2.3_spmd.sunk | while | flops 12587010 | bytes 278637 | solution.py:57
  289.7 8.3 %collective-permute-start = (f32[32,128]{1,0:T(8,128)S(1)}, f32[32,128]{1,0:T(8,128)S(1)}, u32[]{:S(2)}, u32[]{:S(2)}) collective-permute-start(f32[32,128]{1,0:T(8,128)S(1)} %get-tuple-element.162), channel_id=1, source_target_pairs={{0,64},{64,128},{128,192},{192,256},{256,320},{320,384},{384,448},... | collective-permute-start | bytes 49160 | tf_op jit(solution)/shard_map/while/body/eval_jaxpr/ppermute | solution.py:10
  298.0 0.8 collective-permute-done
  299.3 4.2 collective-permute-start
  303.5 0.8 collective-permute-done
  304.8 4.2 collective-permute-start
  309.0 0.8 collective-permute-done
  310.3 4.2 collective-permute-start
  314.5 0.8 collective-permute-done
  315.8 4.2 collective-permute-start
  320.0 0.8 collective-permute-done
  321.2 4.2 collective-permute-start
  325.5 0.8 collective-permute-done
  326.7 4.2 collective-permute-start
  331.0 0.8 collective-permute-done
  332.4 38.3 %while.21 = (s32[]{:T(128)}, f32[32,128]{1,0:T(8,128)S(1)}, f32[128,128]{1,0:T(8,128)S(1)}, f32[32,128]{1,0:T(8,128)S(1)}, f32[128,128]{1,0:T(8,128)S(1)}, /*index=5*/s32[]{:T(128)}) while((s32[]{:T(128)}, f32[32,128]{1,0:T(8,128)S(1)}, f32[128,128]{1,0:T(8,128)S(1)}, f32[32,128]{1,0:T(8,128)S(1)}, f32[128,128]{1,0:T(8,128)S(1)}, ...), condition=%wide.region_5.6_spmd, body=%wide.region_4.5_spmd.sunk | while | flops 12587010 | bytes 278637 | solution.py:64
  332.6 3.4 collective-permute-start.1
  336.0 2.2 collective-permute-done.1
  338.6 1.9 collective-permute-start.1
  340.5 3.1 collective-permute-done.1
  344.0 1.9 collective-permute-start.1
  345.9 3.1 collective-permute-done.1
  349.4 1.9 collective-permute-start.1
  351.3 3.1 collective-permute-done.1
  354.8 1.9 collective-permute-start.1
  356.7 3.1 collective-permute-done.1
  360.1 1.9 collective-permute-start.1
  362.1 3.1 collective-permute-done.1
  365.5 1.9 collective-permute-start.1
  367.5 3.1 collective-permute-done.1
  370.8 1.1 stack.4
  371.9 8.7 %all-to-all-start = ((f32[64,32,128]{2,1,0:T(8,128)}), f32[64,32,128]{2,1,0:T(8,128)S(1)}, u32[]{:S(2)}, u32[]{:S(2)}) async-start(f32[64,32,128]{2,1,0:T(8,128)} %stack.4), calls=%async_computation.1 | async-start | bytes 2097152 | tf_op jit(solution)/shard_map/all_to_all | solution.py:66
  380.7 30.5 %all-to-all-done = f32[64,32,128]{2,1,0:T(8,128)S(1)} async-done(((f32[64,32,128]{2,1,0:T(8,128)}), f32[64,32,128]{2,1,0:T(8,128)S(1)}, u32[]{:S(2)}, u32[]{:S(2)}) %all-to-all-start) | async-done | bytes 1048608 | tf_op jit(solution)/shard_map/all_to_all | solution.py:66
  411.2 2.6 copy.26
  413.8 9.6 %gather_fusion = f32[3584,32]{1,0:T(8,128)} fusion(f32[32,8192]{0,1:T(8,128)} %bitcast.99, s32[4096]{0:T(1024)S(1)} %pad_clamp_fusion), kind=kCustom, calls=%fused_computation | custom fusion | bytes 931840 | tf_op jit(solution)/shard_map/jit(_take)/gather | solution.py:68
  423.4 2.0 copy.27
  425.4 1.7 fusion.21
  427.1 1.7 fusion.15
  429.1 0.8 reshape.82
  (58 shorter events, 6.2 us)
Async XLA Ops:
  7.2 6.5 %copy-start = (f32[1,28,128,128]{3,2,1,0:T(8,128)S(1)}, f32[1,28,128,128]{3,2,1,0:T(8,128)}, u32[]{:S(2)}) copy-start(f32[1,28,128,128]{3,2,1,0:T(8,128)} %param.15) | copy-start | bytes 5505028
  7.2 281.3 %reduce-scatter.2.cloned.1.call-start = ((), (), s32[]{:S(2)}) async-start(), calls=%async_computation.2 | async-start | bytes 4259840 | tf_op jit(solution)/shard_map/reduce_scatter | solution.py:48
  16.6 1.9 copy-start.7
  16.6 1.9 copy-start.5
  41.6 0.7 copy-start.6
  41.6 247.8 %copy-start.1 = (f32[1,1,128,128]{3,2,1,0:T(8,128)S(1)}, f32[1,1,128,128]{3,2,1,0:T(8,128)}, u32[]{:S(2)}) copy-start(f32[1,1,128,128]{3,2,1,0:T(8,128)} %param.18) | copy-start | bytes 196612
  41.6 248.1 %copy-start.3 = (f32[1,1,128,128]{3,2,1,0:T(8,128)S(1)}, f32[1,1,128,128]{3,2,1,0:T(8,128)}, u32[]{:S(2)}) copy-start(f32[1,1,128,128]{3,2,1,0:T(8,128)} %param.19) | copy-start | bytes 196612
  289.7 9.2 %collective-permute-start = (f32[32,128]{1,0:T(8,128)S(1)}, f32[32,128]{1,0:T(8,128)S(1)}, u32[]{:S(2)}, u32[]{:S(2)}) collective-permute-start(f32[32,128]{1,0:T(8,128)S(1)} %get-tuple-element.162), channel_id=1, source_target_pairs={{0,64},{64,128},{128,192},{192,256},{256,320},{320,384},{384,448},... | collective-permute-start | bytes 49160 | tf_op jit(solution)/shard_map/while/body/eval_jaxpr/ppermute | solution.py:10
  299.3 5.1 %collective-permute-start = (f32[32,128]{1,0:T(8,128)S(1)}, f32[32,128]{1,0:T(8,128)S(1)}, u32[]{:S(2)}, u32[]{:S(2)}) collective-permute-start(f32[32,128]{1,0:T(8,128)S(1)} %get-tuple-element.162), channel_id=1, source_target_pairs={{0,64},{64,128},{128,192},{192,256},{256,320},{320,384},{384,448},... | collective-permute-start | bytes 49160 | tf_op jit(solution)/shard_map/while/body/eval_jaxpr/ppermute | solution.py:10
  304.8 5.1 %collective-permute-start = (f32[32,128]{1,0:T(8,128)S(1)}, f32[32,128]{1,0:T(8,128)S(1)}, u32[]{:S(2)}, u32[]{:S(2)}) collective-permute-start(f32[32,128]{1,0:T(8,128)S(1)} %get-tuple-element.162), channel_id=1, source_target_pairs={{0,64},{64,128},{128,192},{192,256},{256,320},{320,384},{384,448},... | collective-permute-start | bytes 49160 | tf_op jit(solution)/shard_map/while/body/eval_jaxpr/ppermute | solution.py:10
  310.3 5.1 %collective-permute-start = (f32[32,128]{1,0:T(8,128)S(1)}, f32[32,128]{1,0:T(8,128)S(1)}, u32[]{:S(2)}, u32[]{:S(2)}) collective-permute-start(f32[32,128]{1,0:T(8,128)S(1)} %get-tuple-element.162), channel_id=1, source_target_pairs={{0,64},{64,128},{128,192},{192,256},{256,320},{320,384},{384,448},... | collective-permute-start | bytes 49160 | tf_op jit(solution)/shard_map/while/body/eval_jaxpr/ppermute | solution.py:10
  315.8 5.1 %collective-permute-start = (f32[32,128]{1,0:T(8,128)S(1)}, f32[32,128]{1,0:T(8,128)S(1)}, u32[]{:S(2)}, u32[]{:S(2)}) collective-permute-start(f32[32,128]{1,0:T(8,128)S(1)} %get-tuple-element.162), channel_id=1, source_target_pairs={{0,64},{64,128},{128,192},{192,256},{256,320},{320,384},{384,448},... | collective-permute-start | bytes 49160 | tf_op jit(solution)/shard_map/while/body/eval_jaxpr/ppermute | solution.py:10
  321.2 5.1 %collective-permute-start = (f32[32,128]{1,0:T(8,128)S(1)}, f32[32,128]{1,0:T(8,128)S(1)}, u32[]{:S(2)}, u32[]{:S(2)}) collective-permute-start(f32[32,128]{1,0:T(8,128)S(1)} %get-tuple-element.162), channel_id=1, source_target_pairs={{0,64},{64,128},{128,192},{192,256},{256,320},{320,384},{384,448},... | collective-permute-start | bytes 49160 | tf_op jit(solution)/shard_map/while/body/eval_jaxpr/ppermute | solution.py:10
  326.7 5.1 %collective-permute-start = (f32[32,128]{1,0:T(8,128)S(1)}, f32[32,128]{1,0:T(8,128)S(1)}, u32[]{:S(2)}, u32[]{:S(2)}) collective-permute-start(f32[32,128]{1,0:T(8,128)S(1)} %get-tuple-element.162), channel_id=1, source_target_pairs={{0,64},{64,128},{128,192},{192,256},{256,320},{320,384},{384,448},... | collective-permute-start | bytes 49160 | tf_op jit(solution)/shard_map/while/body/eval_jaxpr/ppermute | solution.py:10
  332.6 5.6 %collective-permute-start.1 = (f32[32,128]{1,0:T(8,128)S(1)}, f32[32,128]{1,0:T(8,128)S(1)}, u32[]{:S(2)}, u32[]{:S(2)}) collective-permute-start(f32[32,128]{1,0:T(8,128)S(1)} %fusion.77), channel_id=1, source_target_pairs={{64,0},{128,64},{192,128},{256,192},{320,256},{384,320},{448,384},... | collective-permute-start | bytes 49160 | tf_op jit(solution)/shard_map/while/body/eval_jaxpr/ppermute | solution.py:10
  338.6 5.1 %collective-permute-start.1 = (f32[32,128]{1,0:T(8,128)S(1)}, f32[32,128]{1,0:T(8,128)S(1)}, u32[]{:S(2)}, u32[]{:S(2)}) collective-permute-start(f32[32,128]{1,0:T(8,128)S(1)} %fusion.77), channel_id=1, source_target_pairs={{64,0},{128,64},{192,128},{256,192},{320,256},{384,320},{448,384},... | collective-permute-start | bytes 49160 | tf_op jit(solution)/shard_map/while/body/eval_jaxpr/ppermute | solution.py:10
  344.0 5.1 %collective-permute-start.1 = (f32[32,128]{1,0:T(8,128)S(1)}, f32[32,128]{1,0:T(8,128)S(1)}, u32[]{:S(2)}, u32[]{:S(2)}) collective-permute-start(f32[32,128]{1,0:T(8,128)S(1)} %fusion.77), channel_id=1, source_target_pairs={{64,0},{128,64},{192,128},{256,192},{320,256},{384,320},{448,384},... | collective-permute-start | bytes 49160 | tf_op jit(solution)/shard_map/while/body/eval_jaxpr/ppermute | solution.py:10
  349.4 5.1 %collective-permute-start.1 = (f32[32,128]{1,0:T(8,128)S(1)}, f32[32,128]{1,0:T(8,128)S(1)}, u32[]{:S(2)}, u32[]{:S(2)}) collective-permute-start(f32[32,128]{1,0:T(8,128)S(1)} %fusion.77), channel_id=1, source_target_pairs={{64,0},{128,64},{192,128},{256,192},{320,256},{384,320},{448,384},... | collective-permute-start | bytes 49160 | tf_op jit(solution)/shard_map/while/body/eval_jaxpr/ppermute | solution.py:10
  354.8 5.1 %collective-permute-start.1 = (f32[32,128]{1,0:T(8,128)S(1)}, f32[32,128]{1,0:T(8,128)S(1)}, u32[]{:S(2)}, u32[]{:S(2)}) collective-permute-start(f32[32,128]{1,0:T(8,128)S(1)} %fusion.77), channel_id=1, source_target_pairs={{64,0},{128,64},{192,128},{256,192},{320,256},{384,320},{448,384},... | collective-permute-start | bytes 49160 | tf_op jit(solution)/shard_map/while/body/eval_jaxpr/ppermute | solution.py:10
  360.1 5.1 %collective-permute-start.1 = (f32[32,128]{1,0:T(8,128)S(1)}, f32[32,128]{1,0:T(8,128)S(1)}, u32[]{:S(2)}, u32[]{:S(2)}) collective-permute-start(f32[32,128]{1,0:T(8,128)S(1)} %fusion.77), channel_id=1, source_target_pairs={{64,0},{128,64},{192,128},{256,192},{320,256},{384,320},{448,384},... | collective-permute-start | bytes 49160 | tf_op jit(solution)/shard_map/while/body/eval_jaxpr/ppermute | solution.py:10
  365.5 5.1 %collective-permute-start.1 = (f32[32,128]{1,0:T(8,128)S(1)}, f32[32,128]{1,0:T(8,128)S(1)}, u32[]{:S(2)}, u32[]{:S(2)}) collective-permute-start(f32[32,128]{1,0:T(8,128)S(1)} %fusion.77), channel_id=1, source_target_pairs={{64,0},{128,64},{192,128},{256,192},{320,256},{384,320},{448,384},... | collective-permute-start | bytes 49160 | tf_op jit(solution)/shard_map/while/body/eval_jaxpr/ppermute | solution.py:10
  370.8 43.0 %copy-start.4 = (f32[32,128]{1,0:T(8,128)}, f32[32,128]{1,0:T(8,128)S(1)}, u32[]{:S(2)}) copy-start(f32[32,128]{1,0:T(8,128)S(1)} %get-tuple-element.57) | copy-start | bytes 49156
  371.9 39.3 %all-to-all-start = ((f32[64,32,128]{2,1,0:T(8,128)}), f32[64,32,128]{2,1,0:T(8,128)S(1)}, u32[]{:S(2)}, u32[]{:S(2)}) async-start(f32[64,32,128]{2,1,0:T(8,128)} %stack.4), calls=%async_computation.1 | async-start | bytes 2097152 | tf_op jit(solution)/shard_map/all_to_all | solution.py:66
  425.4 1.7 copy-start.2
Sparse Core Ops, SparseCore 0:
  41.7 246.7 reduce-scatter.1
